TPU v7x, 32 devices: a whole 2x2x4 slice. The times are simulated.
32 devices in a mesh: scen: 2 (over y), lag: 4 (over z), elem: 4 (over x, core).
Axes of the slice: x: 2, y: 2, z: 4, core: 2. Of those that a mesh axis runs over, the one named last changes fastest.
Arguments:
- kernel: bfloat16 [16, 2048, 2048], P('lag', 'elem'), may hold values from -0.03125 to 0.03125
- past_rate: bfloat16 [16, 256, 2048], P('lag', 'scen'), parts along dimension 1, may hold values from 0 to 1
- loading: float32 [256, 2048], P('scen', 'elem'), parts along dimension 0, may hold values from -6 to 6
- initial_slip: float32 [256, 2048], P('scen', 'elem'), parts along dimension 0, may hold values from 0 to 1
- peak_strength: float32 [2048], P('elem'), may hold values from 0.5 to 2
- cohesive_flags: int32 [2048], P('elem'), may hold values 0 or 1
- patch_start: int32 [256], P('scen'), parts along dimension 0, may hold values from 0 to 1920
- rad_kernel: bfloat16 [16, 1024, 512], P(None, ('lag', 'elem')), may hold values from -0.0625 to 0.0625
- block_map: int32 [16, 4], P(('lag', 'elem')), may hold values from 0 to 15, all different within a row
Outputs:
- slip_now: float32 [256, 2048], P(('scen', 'lag'), 'elem'), parts along dimension 0
- traction: float32 [256, 2048], P(('scen', 'lag'), 'elem'), parts along dimension 0
- motion: float32 [256, 1024], P('scen', ('lag', 'elem')), parts along dimension 0
There are 2 independent parts, one for each index of `scen`. A program takes and returns all parts, laid end to end along the dimension named above; an argument that names none is the same for every part. Nothing has to cross between parts.
Inputs may be any that keep to these rules, and one draw needn't show every extreme that they name: `block_map`: each row names 4 different source blocks, and every block is named by some row.
All inputs are finite; a program needn't handle non-finite values. No bound on the sum of `cohesive_flags` on one device may be relied on, other than what follows from the above.
Results may differ from a plain program's by a relative error of at most 0.0018.
Values may be sent and summed in bfloat16 or wider, within the bound.
A program may use at most 128 MiB of HBM per device.

v0:
```python
import jax
import jax.numpy as jnp
from jax import lax
from jax.sharding import PartitionSpec as P

STEPS = 4
SBLK = 16
PATCH = 128


OVERSTRESS = 2.0
WEAKEN = 0.5
CRITICAL = 0.5


def from_root(value, axis, root):
    mine = lax.axis_index(axis) == root
    return lax.psum(jnp.where(mine, value, jnp.zeros_like(value)), axis)


def shifted(value, axis, steps):
    count = lax.axis_size(axis)
    first, last = (max(0, -steps), min(count, count - steps))
    return lax.ppermute(value, axis, [(source, source + steps) for source in range(first, last)])


def select_blocks(rate_block, sources):
    grouped = rate_block.reshape(
        rate_block.shape[0], rate_block.shape[1], SBLK, rate_block.shape[2] // SBLK
    )
    chosen = jnp.take(grouped, sources, axis=2)
    return chosen.reshape(rate_block.shape[0], rate_block.shape[1], -1)


def radiate(summed, rate_block, rad_kernel, first_lag):
    kernel_slab = rad_kernel[first_lag : first_lag + rate_block.shape[0]]
    return summed + jnp.einsum(
        "msk,mrk->sr", rate_block, kernel_slab, preferred_element_type=jnp.float32
    )


def lag_terms(history, kernel):
    return lax.dot_general(
        history, kernel, (((0, 2), (0, 2)), ((), ())), preferred_element_type=jnp.float32
    )


def on_device(
    kernel,
    past_rate,
    loading,
    initial_slip,
    peak_strength,
    cohesive_flags,
    patch_start,
    rad_kernel,
    block_map,
):
    lag_depth = past_rate.shape[0]
    scenarios = past_rate.shape[1]
    columns = kernel.shape[1]
    lag_devices = lax.axis_size("lag")
    lag_position = lax.axis_index("lag")
    first_column = lax.axis_index("elem") * columns
    positions = first_column + jnp.arange(columns, dtype=jnp.int32)[None, :]
    first_cell = patch_start[:, None]
    inside = jnp.where(
        (positions >= first_cell) & (positions < first_cell + PATCH), 1.0, 0.0
    ).astype(jnp.float32)
    driven = loading + OVERSTRESS * inside
    weakening = WEAKEN * cohesive_flags.astype(jnp.float32)
    share_rows = scenarios // lag_devices
    first_row = lag_position * share_rows
    sources = block_map[0]
    motion = jnp.zeros((scenarios, rad_kernel.shape[1]), jnp.float32)
    needed = rad_kernel.shape[0] - STEPS
    for root_index in range(-(-needed // lag_depth)):
        old_block = from_root(past_rate, "lag", root_index)
        motion = radiate(
            motion, select_blocks(old_block, sources), rad_kernel, STEPS + root_index * lag_depth
        )
    driven = lax.dynamic_slice_in_dim(driven, first_row, share_rows, 0)
    slip_now = lax.dynamic_slice_in_dim(initial_slip, first_row, share_rows, 0)
    history = past_rate
    new_rates = []
    traction = driven
    for moment in range(STEPS):
        partial_value = lag_terms(history, kernel)
        traction = driven + lax.psum_scatter(partial_value, "lag", scatter_dimension=0, tiled=True)
        strength = peak_strength * (1.0 - weakening * slip_now / (slip_now + CRITICAL))
        slip_rate = jnp.maximum(traction - strength, 0.0).astype(jnp.bfloat16)
        slip_now = slip_now + slip_rate.astype(jnp.float32)
        gathered = lax.all_gather(slip_rate, "elem", axis=1, tiled=True)
        gathered = lax.all_gather(gathered, "lag", axis=0, tiled=True)
        new_rates.append(gathered)
        if moment + 1 < STEPS:
            arriving = shifted(history[lag_depth - 1 :], "lag", 1)
            newest = jnp.where(lag_position == 0, gathered[None], arriving)
            history = jnp.concatenate([newest, history[: lag_depth - 1]], 0)
    motion = radiate(motion, select_blocks(jnp.stack(new_rates[::-1]), sources), rad_kernel, 0)
    return (slip_now, traction, motion)


def solution(mesh):
    return jax.shard_map(
        on_device,
        mesh=mesh,
        in_specs=(
            P("lag", "elem", None),
            P("lag", "scen", None),
            P("scen", "elem"),
            P("scen", "elem"),
            P("elem"),
            P("elem"),
            P("scen"),
            P(None, ("lag", "elem"), None),
            P(("lag", "elem"), None),
        ),
        out_specs=(
            P(("scen", "lag"), "elem"),
            P(("scen", "lag"), "elem"),
            P("scen", ("lag", "elem")),
        ),
        check_vma=False,
    )
```

profile of v0, /device:TPU:19, one launch (start us, length us, event | category | flops | bytes accessed | tf_op | source)
XLA Modules:
  0.0 444.0 jit_solution(12647336407231489381)
XLA Ops:
  7.2 7.8 %convolution_bitcast_fusion = f32[128,512]{1,0:T(8,128)} fusion(bf16[4,128,2048]{2,1,0:T(8,128)(2,1)} %param.12, bf16[4,512,2048]{2,1,0:T(8,128)(2,1)} %param.11), kind=kOutput, calls=%fused_computation.26 | convolution fusion | flops 1073741824 | bytes 10747904 | tf_op jit(solution)/shard_map/dot_general | solution.py:43
  15.1 1.2 fusion.31
  16.4 3.3 collective-permute-start
  19.8 1.3 slice.35
  21.2 12.3 %reduce-scatter.5.cloned.1.call-done = f32[32,512]{1,0:T(8,128)} async-done(((f32[128,512]{1,0:T(8,128)}), f32[32,512]{1,0:T(8,128)}) %reduce-scatter.5.cloned.1.call-update) | async-done | bytes 65552 | tf_op jit(solution)/shard_map/reduce_scatter | solution.py:89
  33.5 1.1 maximum_convert_fusion.3
  34.6 8.4 %all_gather.24 = bf16[32,2048]{1,0:T(8,128)(2,1)S(1)} all-gather(bf16[32,512]{1,0:T(8,128)(2,1)S(1)} %maximum_convert_fusion.3), channel_id=1, replica_groups=mesh['scen'=2,'lag'=4,'elem'=4] {'elem'}, dimensions={1}, use_global_device_ids=true | all-gather | bytes 163840 | tf_op jit(solution)/shard_map/all_gather | solution.py:93
  43.0 13.3 %all_gather.25 = bf16[128,2048]{1,0:T(8,128)(2,1)S(1)} all-gather(bf16[32,2048]{1,0:T(8,128)(2,1)S(1)} %all_gather.24), channel_id=1, replica_groups=mesh['scen'=2,'lag'=4,'elem'=4] {'lag'}, dimensions={0}, use_global_device_ids=true | all-gather | bytes 655360 | tf_op jit(solution)/shard_map/all_gather | solution.py:94
  56.2 0.8 copy-done.4
  57.1 1.1 bitcast_select_fusion.2
  58.2 0.8 copy-done.15
  59.0 7.0 %fusion.14 = f32[128,512]{1,0:T(8,128)} fusion(bf16[4,512,2048]{2,1,0:T(8,128)(2,1)} %param.11, bf16[3,128,2048]{2,1,0:T(8,128)(2,1)S(1)} %copy-done.12, bf16[1,128,2048]{2,1,0:T(8,128)(2,1)S(1)} %bitcast_select_fusion.2), kind=kOutput, calls=%fused_computation.23 | convolution fusion | flops 1074790400 | bytes 10747904 | tf_op jit(solution)/shard_map/dot_general | solution.py:43
  66.0 3.2 collective-permute-start.1
  69.2 16.4 %reduce-scatter.7.cloned.1.call-done = f32[32,512]{1,0:T(8,128)} async-done(((f32[128,512]{1,0:T(8,128)}), f32[32,512]{1,0:T(8,128)}) %reduce-scatter.7.cloned.1.call-update) | async-done | bytes 65552 | tf_op jit(solution)/shard_map/reduce_scatter | solution.py:89
  85.6 1.1 maximum_convert_fusion.2
  86.7 7.7 %all_gather.26 = bf16[32,2048]{1,0:T(8,128)(2,1)S(1)} all-gather(bf16[32,512]{1,0:T(8,128)(2,1)S(1)} %maximum_convert_fusion.2), channel_id=1, replica_groups=mesh['scen'=2,'lag'=4,'elem'=4] {'elem'}, dimensions={1}, use_global_device_ids=true | all-gather | bytes 163840 | tf_op jit(solution)/shard_map/all_gather | solution.py:93
  94.4 13.3 %all_gather.27 = bf16[128,2048]{1,0:T(8,128)(2,1)S(1)} all-gather(bf16[32,2048]{1,0:T(8,128)(2,1)S(1)} %all_gather.26), channel_id=1, replica_groups=mesh['scen'=2,'lag'=4,'elem'=4] {'lag'}, dimensions={0}, use_global_device_ids=true | all-gather | bytes 655360 | tf_op jit(solution)/shard_map/all_gather | solution.py:94
  107.7 0.8 copy-done.6
  108.4 1.1 bitcast_select_fusion.1
  109.5 0.8 copy-done.18
  110.4 7.0 %fusion.17 = f32[128,512]{1,0:T(8,128)} fusion(bf16[4,512,2048]{2,1,0:T(8,128)(2,1)} %param.11, bf16[3,128,2048]{2,1,0:T(8,128)(2,1)S(1)} %copy-done.13, bf16[1,128,2048]{2,1,0:T(8,128)(2,1)S(1)} %copy-done.16, bf16[1,128,2048]{2,1,0:T(8,128)(2,1)S(1)} %bitcast_select_fusion.1), kind=kOutput, calls=%fused_computation.24 | convolution fusion | flops 1075838976 | bytes 11272192 | tf_op jit(solution)/shard_map/dot_general | solution.py:43
  117.4 2.7 collective-permute-start.2
  120.1 2.5 copy.16
  122.7 14.1 %reduce-scatter.9.cloned.1.call-done = f32[32,512]{1,0:T(8,128)} async-done(((f32[128,512]{1,0:T(8,128)}), f32[32,512]{1,0:T(8,128)}) %reduce-scatter.9.cloned.1.call-update) | async-done | bytes 65552 | tf_op jit(solution)/shard_map/reduce_scatter | solution.py:89
  136.8 1.1 maximum_convert_fusion.1
  137.9 7.6 %all_gather.28 = bf16[32,2048]{1,0:T(8,128)(2,1)S(1)} all-gather(bf16[32,512]{1,0:T(8,128)(2,1)S(1)} %maximum_convert_fusion.1), channel_id=1, replica_groups=mesh['scen'=2,'lag'=4,'elem'=4] {'elem'}, dimensions={1}, use_global_device_ids=true | all-gather | bytes 163840 | tf_op jit(solution)/shard_map/all_gather | solution.py:93
  145.5 13.3 %all_gather.29 = bf16[128,2048]{1,0:T(8,128)(2,1)S(1)} all-gather(bf16[32,2048]{1,0:T(8,128)(2,1)S(1)} %all_gather.28), channel_id=1, replica_groups=mesh['scen'=2,'lag'=4,'elem'=4] {'lag'}, dimensions={0}, use_global_device_ids=true | all-gather | bytes 655360 | tf_op jit(solution)/shard_map/all_gather | solution.py:94
  158.8 0.8 copy-done.8
  159.6 1.1 bitcast_select_fusion
  160.7 7.1 %fusion.20 = f32[128,512]{1,0:T(8,128)} fusion(bf16[4,512,2048]{2,1,0:T(8,128)(2,1)} %param.11, bf16[1,128,2048]{2,1,0:T(8,128)(2,1)S(1)} %copy-done.19, bf16[3,128,2048]{2,1,0:T(8,128)(2,1)S(1)} %copy-done.14, bf16[1,128,2048]{2,1,0:T(8,128)(2,1)S(1)} %copy-done.17, bf16[1,128,2048]{2,1,0:T(8,128)(2,1)S(1)} %bitcast_select_fusion), kind=kOutput, calls=%fused_computation.25 | convolution fusion | flops 1076887552 | bytes 11796480 | tf_op jit(solution)/shard_map/dot_general | solution.py:43
  167.9 0.2 all-reduce.3.cloned.1.call-start
  168.1 2.8 broadcast_select_fusion
  170.9 4.0 copy.17
  174.9 4.1 copy.21
  179.0 2.7 copy.25
  181.7 0.6 copy-done.24
  182.4 0.4 copy-done.5
  182.8 0.1 copy.41
  182.9 1.0 copy.31
  183.9 0.1 copy.40
  184.0 0.9 copy.30
  184.9 0.1 copy.39
  185.0 0.9 copy.29
  185.9 0.7 reduce-scatter.11.cloned.1.call-done
  186.7 1.7 convert_add_fusion
  188.3 8.3 %all_gather.30 = bf16[32,2048]{1,0:T(8,128)(2,1)S(1)} all-gather(bf16[32,512]{1,0:T(8,128)(2,1)S(1)} %get-tuple-element.8), channel_id=1, replica_groups=mesh['scen'=2,'lag'=4,'elem'=4] {'elem'}, dimensions={1}, use_global_device_ids=true | all-gather | bytes 163840 | tf_op jit(solution)/shard_map/all_gather | solution.py:93
  196.7 22.0 %all_gather.31 = bf16[128,2048]{1,0:T(8,128)(2,1)S(1)} all-gather(bf16[32,2048]{1,0:T(8,128)(2,1)S(1)} %all_gather.30), channel_id=1, replica_groups=mesh['scen'=2,'lag'=4,'elem'=4] {'lag'}, dimensions={0}, use_global_device_ids=true | all-gather | bytes 655360 | tf_op jit(solution)/shard_map/all_gather | solution.py:94
  218.6 0.1 copy.38
  218.7 0.1 copy.28
  218.9 1.5 pad_maximum_fusion.4
  220.4 1.5 gather_fusion.3
  221.8 199.7 %all-reduce.3.cloned.1.call-done = (bf16[4,128,16,128]{3,1,2,0:T(8,128)(2,1)}, bf16[4,128,16,128]{3,1,2,0:T(8,128)(2,1)}, bf16[4,128,16,128]{3,1,2,0:T(8,128)(2,1)}) async-done(((bf16[4,128,16,128]{3,1,2,0:T(8,128)(2,1)}, bf16[4,128,16,128]{3,1,2,0:T(8,128)(2,1)}, bf16[4,128,16,128]{3,1,2,0:T(8,128)(2,1)}), (bf16[4,128,16,128]{3,1,2,0:T(8,128)(2,1)}, bf16[4,128,16,128]{3,1,2,0:T(8,128)(2,1)}, ...) | async-done | bytes 6291472 | tf_op jit(solution)/shard_map/psum | solution.py:18
  421.6 3.0 gather_fusion
  424.6 3.0 gather_fusion.1
  427.6 3.0 gather_fusion.2
  430.6 1.8 select_bitcast_fusion
  432.3 1.0 copy.18
  433.3 1.0 copy.22
  434.4 0.3 copy.26
  434.6 0.3 copy.32
  434.9 0.2 convolution_bitcast_fusion.4
  435.2 1.3 fusion.25
  436.4 0.2 fusion.24
  436.7 0.8 fusion.23
  (63 shorter events, 0.5 us)
Async XLA Ops:
  7.2 427.8 %copy-start = (bf16[16,64,512]{2,1,0:T(8,128)(2,1)S(1)}, bf16[16,64,512]{2,1,0:T(8,128)(2,1)}, u32[]{:S(2)}) copy-start(bf16[16,64,512]{2,1,0:T(8,128)(2,1)} %param.18) | copy-start | bytes 3145732
  7.2 7.9 %copy-start.1 = (bf16[4,128,2048]{2,1,0:T(8,128)(2,1)S(1)}, bf16[4,128,2048]{2,1,0:T(8,128)(2,1)}, u32[]{:S(2)}) copy-start(bf16[4,128,2048]{2,1,0:T(8,128)(2,1)} %param.12) | copy-start | bytes 6291460
  7.2 26.3 %reduce-scatter.5.cloned.1.call-start = ((), (), s32[]{:S(2)}) async-start(), calls=%async_computation.4 | async-start | bytes 327680 | tf_op jit(solution)/shard_map/reduce_scatter | solution.py:89
  15.0 4.7 %copy-start.23 = (s32[128]{0:T(128)S(1)}, s32[128]{0:T(128)}, u32[]{:S(2)}) copy-start(s32[128]{0:T(128)} %param.17) | copy-start | bytes 1540
  15.0 4.7 %copy-start.22 = (s32[512]{0:T(512)S(1)}, s32[512]{0:T(512)}, u32[]{:S(2)}) copy-start(s32[512]{0:T(512)} %param.16) | copy-start | bytes 6148
  15.1 70.5 %reduce-scatter.7.cloned.1.call-start = ((), (), s32[]{:S(2)}) async-start(), calls=%async_computation.5 | async-start | bytes 327680 | tf_op jit(solution)/shard_map/reduce_scatter | solution.py:89
  16.4 17.1 %copy-start.20 = (f32[128,512]{1,0:T(8,128)S(1)}, f32[128,512]{1,0:T(8,128)}, u32[]{:S(2)}) copy-start(f32[128,512]{1,0:T(8,128)} %param.14) | copy-start | bytes 786436
  16.4 17.1 %copy-start.21 = (f32[512]{0:T(512)S(1)}, f32[512]{0:T(512)}, u32[]{:S(2)}) copy-start(f32[512]{0:T(512)} %param.15) | copy-start | bytes 6148
  16.4 39.9 %collective-permute-start = (bf16[1,128,2048]{2,1,0:T(8,128)(2,1)}, bf16[1,128,2048]{2,1,0:T(8,128)(2,1)}, u32[]{:S(2)}, u32[]{:S(2)}) collective-permute-start(bf16[1,128,2048]{2,1,0:T(8,128)(2,1)} %get-tuple-element.15), channel_id=1, source_target_pairs={{0,4},{4,8},{8,12},{1,5},{5,9},{9,13},{2,6},{6,10},{10,14},{3,7},{... | collective-permute-start | bytes 1572872 | tf_op jit(solution)/shard_map/ppermute | solution.py:24
  33.5 25.5 %copy-start.12 = (bf16[3,128,2048]{2,1,0:T(8,128)(2,1)S(1)}, bf16[3,128,2048]{2,1,0:T(8,128)(2,1)}, u32[]{:S(2)}) copy-start(bf16[3,128,2048]{2,1,0:T(8,128)(2,1)} %slice.35) | copy-start | bytes 4718596
  56.2 0.8 copy-start.4
  58.2 0.8 copy-start.15
  66.0 70.8 %reduce-scatter.9.cloned.1.call-start = ((), (), s32[]{:S(2)}) async-start(), calls=%async_computation.6 | async-start | bytes 327680 | tf_op jit(solution)/shard_map/reduce_scatter | solution.py:89
  66.0 41.6 %collective-permute-start.1 = (bf16[1,128,2048]{2,1,0:T(8,128)(2,1)}, bf16[1,128,2048]{2,1,0:T(8,128)(2,1)}, u32[]{:S(2)}, u32[]{:S(2)}) collective-permute-start(bf16[1,128,2048]{2,1,0:T(8,128)(2,1)} %get-tuple-element.14), channel_id=1, source_target_pairs={{0,4},{4,8},{8,12},{1,5},{5,9},{9,13},{2,6},{6,10},{10,14},{3,7},{... | collective-permute-start | bytes 1572872 | tf_op jit(solution)/shard_map/ppermute | solution.py:24
  85.6 24.8 %copy-start.13 = (bf16[3,128,2048]{2,1,0:T(8,128)(2,1)S(1)}, bf16[3,128,2048]{2,1,0:T(8,128)(2,1)}, u32[]{:S(2)}) copy-start(bf16[3,128,2048]{2,1,0:T(8,128)(2,1)} %slice.35) | copy-start | bytes 4718596
  85.6 24.8 %copy-start.16 = (bf16[1,128,2048]{2,1,0:T(8,128)(2,1)S(1)}, bf16[1,128,2048]{2,1,0:T(8,128)(2,1)}, u32[]{:S(2)}) copy-start(bf16[1,128,2048]{2,1,0:T(8,128)(2,1)} %copy-done.15) | copy-start | bytes 1572868
  107.6 0.8 copy-start.6
  109.5 0.8 copy-start.18
  117.4 69.3 %reduce-scatter.11.cloned.1.call-start = ((), (), s32[]{:S(2)}) async-start(), calls=%async_computation.7 | async-start | bytes 327680 | tf_op jit(solution)/shard_map/reduce_scatter | solution.py:89
  117.4 41.4 %collective-permute-start.2 = (bf16[1,128,2048]{2,1,0:T(8,128)(2,1)}, bf16[1,128,2048]{2,1,0:T(8,128)(2,1)}, u32[]{:S(2)}, u32[]{:S(2)}) collective-permute-start(bf16[1,128,2048]{2,1,0:T(8,128)(2,1)} %get-tuple-element.13), channel_id=1, source_target_pairs={{0,4},{4,8},{8,12},{1,5},{5,9},{9,13},{2,6},{6,10},{10,14},{3,7},{... | collective-permute-start | bytes 1572872 | tf_op jit(solution)/shard_map/ppermute | solution.py:24
  136.8 23.9 %copy-start.14 = (bf16[3,128,2048]{2,1,0:T(8,128)(2,1)S(1)}, bf16[3,128,2048]{2,1,0:T(8,128)(2,1)}, u32[]{:S(2)}) copy-start(bf16[3,128,2048]{2,1,0:T(8,128)(2,1)} %slice.35) | copy-start | bytes 4718596
  136.8 23.9 %copy-start.17 = (bf16[1,128,2048]{2,1,0:T(8,128)(2,1)S(1)}, bf16[1,128,2048]{2,1,0:T(8,128)(2,1)}, u32[]{:S(2)}) copy-start(bf16[1,128,2048]{2,1,0:T(8,128)(2,1)} %copy-done.15) | copy-start | bytes 1572868
  136.8 23.9 %copy-start.19 = (bf16[1,128,2048]{2,1,0:T(8,128)(2,1)S(1)}, bf16[1,128,2048]{2,1,0:T(8,128)(2,1)}, u32[]{:S(2)}) copy-start(bf16[1,128,2048]{2,1,0:T(8,128)(2,1)} %copy-done.18) | copy-start | bytes 1572868
  158.8 0.8 copy-start.8
  160.7 7.4 %copy-start.2 = (bf16[4,128,2048]{1,2,0:T(8,128)(2,1)S(1)}, bf16[4,128,2048]{1,2,0:T(8,128)(2,1)}, u32[]{:S(2)}) copy-start(bf16[4,128,2048]{1,2,0:T(8,128)(2,1)} %copy.16) | copy-start | bytes 6291460
  167.9 253.7 %all-reduce.3.cloned.1.call-start = ((), (), s32[]{:S(2)}) async-start(), calls=%async_computation.8 | async-start | bytes 12582912 | tf_op jit(solution)/shard_map/psum | solution.py:18
  174.9 4.1 copy-start.3
  181.7 0.7 copy-start.24
  181.7 1.1 copy-start.5
  182.3 1.5 copy-start.7
  182.7 2.1 copy-start.9
  186.7 32.2 %copy-start.11 = (bf16[1,128,16,128]{3,1,2,0:T(8,128)(2,1)S(1)}, bf16[1,128,16,128]{3,1,2,0:T(8,128)(2,1)}, u32[]{:S(2)}) copy-start(bf16[1,128,16,128]{3,1,2,0:T(8,128)(2,1)} %copy.29) | copy-start | bytes 1572868
  433.3 1.6 copy-start.10
Sparse Core Ops, SparseCore 0:
  15.2 18.2 reduce-scatter.4
  66.1 19.4 reduce-scatter.6
  117.5 19.2 reduce-scatter.8
  168.0 18.5 reduce-scatter.10
  189.1 232.4 all-reduce.2
where the time goes:
time: 448 us; the launch traced here: 444 us
  waiting for transfers between devices  243 us (54%)
  blocking collectives  93.8 us (21%)
  local copies, waits for them, and re-layouts  37.4 us (8%)
  matrix products  31.5 us (7%)
  other arithmetic  14.3 us (3%)
  between operations  14.1 us (3%)
  starting transfers between devices  9.53 us (2%)
    psum x1, waiting for transfers between devices, from_root(): return lax.psum(jnp.where(mine, value, jnp.zeros_like(value)), axis)  200 us
    all_gather x4, blocking collectives, on_device(): gathered = lax.all_gather(gathered, 'lag', axis=0, tiled=True)  61.8 us
    reduce_scatter x4, waiting for transfers between devices, on_device(): lax.psum_scatter(partial_value, 'lag', scatter_dimension=0, tiled=True)  43.6 us
    all_gather x4, blocking collectives, on_device(): gathered = lax.all_gather(slip_rate, 'elem', axis=1, tiled=True)  32 us
    dot_general x4, matrix products, lag_terms(): lax.dot_general(history, kernel, (((0, 2), (0, 2)), ((), ())), preferred_...  28.9 us
    reshape x3, local copies, waits for them, and re-layouts, select_blocks(): rate_block.reshape(rate_block.shape[0], rate_block.shape[1], SBLK, rate_b...  10.7 us
    gather x4, local copies, waits for them, and re-layouts, select_blocks(): chosen = jnp.take(grouped, sources, axis=2)  10.4 us
    ppermute x3, starting transfers between devices, shifted(): lax.ppermute(value, axis, [(source, source + steps) for source in range(f...  9.15 us
  transfers between devices with their start and end apart: 8, of which 5 were waited for; matrix products, arithmetic and copies ran while one was open for 7% of the time, Pallas kernels for 0%

commit v1 on v0

v1 whole, which is shorter than its diff:
```python
import functools

import jax
import jax.numpy as jnp
from jax import lax
from jax.experimental import pallas as pl
from jax.experimental.pallas import tpu as pltpu
from jax.sharding import PartitionSpec as P

STEPS = 4
SBLK = 16
PATCH = 128
OVERSTRESS = 2.0
WEAKEN = 0.5
CRITICAL = 0.5

CHUNKS = 2


def flip(e, bits):
    bit = 1
    while bit <= bits:
        if bits & bit:
            e = e + bit - 2 * bit * ((e // bit) % 2)
        bit *= 2
    return e


def nt(a, b):
    return lax.dot_general(a, b, (((1,), (1,)), ((), ())), preferred_element_type=jnp.float32)


def body(
    n_lag, n_elem, near,
    kernel_h, past_h, loading, initial, peak, flags, patch, rad_h, bpad,
    slip_out, trac_out, motion_out,
    kern, hist, rad, radin, bin_v, psum, pin, slip, trs, trin, mpart, min_,
    ksem, psem, rsem,
    z_s, z_r, g_s, g_r, p_s, p_r, v_s, v_r, rad_s, rad_r, bm_s, bm_r, t_s, t_r, m_s, m_r,
):
    depth, cols, _ = kern.shape
    scen = psum.shape[1]
    NEW = STEPS - 1 + depth
    crow = scen // CHUNKS
    rows = scen // n_lag
    handlers = (rad_h.shape[0] - STEPS) // depth
    lag = lax.axis_index("lag")
    elem = lax.axis_index("elem")
    first = lag == 0
    later = lag > 0
    inner = lag < n_lag - 1
    up = lax.rem(lag + 1, n_lag)
    down = lax.rem(lag + n_lag - 1, n_lag)
    bits = []
    bit = n_elem // 2
    while bit:
        bits.append(bit)
        bit //= 2

    pending = []

    def remote(src, dst, ss, rs, **where):
        return pltpu.make_async_remote_copy(
            src_ref=src, dst_ref=dst, send_sem=ss, recv_sem=rs,
            device_id=where, device_id_type=pl.DeviceIdType.MESH)

    def go(desc, cond=None):
        if cond is None:
            desc.start()
        else:
            pl.when(cond)(desc.start)
        pending.append((cond, desc))

    kcopies = [pltpu.make_async_copy(kernel_h.at[i], kern.at[i], ksem.at[i]) for i in range(depth)]
    pcopies = [[pltpu.make_async_copy(past_h.at[i, :, pl.ds(q * cols, cols)], hist.at[STEPS - 1 + i, q], psem.at[i, q])
                for q in range(n_elem)] for i in range(depth)]
    rcopy = pltpu.make_async_copy(rad_h, rad, rsem)
    for i in range(depth):
        for c in pcopies[i]:
            c.start()
        kcopies[i].start()
    rcopy.start()

    barrier = pltpu.get_barrier_semaphore()

    def greet(k, c):
        pl.semaphore_signal(barrier, inc=1, device_id={"lag": lax.rem(lag + k, n_lag)},
                            device_id_type=pl.DeviceIdType.MESH)
        return c

    lax.fori_loop(1, n_lag, greet, 0)
    for b in bits:
        pl.semaphore_signal(barrier, inc=1, device_id={"elem": flip(elem, b)},
                            device_id_type=pl.DeviceIdType.MESH)
    pl.semaphore_wait(barrier, n_lag - 1 + len(bits))

    def stages():
        held = [0]
        out = []
        for b in bits:
            out.append((b, list(held)))
            held = held + [h ^ b for h in held]
        return out

    plan = stages()

    def g_desc(slot, k, n, off):
        b = plan[k][0]
        q = flip(elem, off)
        return remote(hist.at[slot, q], hist.at[slot, q], g_s.at[slot, k, n], g_r.at[slot, k, n],
                      elem=flip(elem, b))

    def g_start(slot, k, cond=None):
        for n, off in enumerate(plan[k][1]):
            go(g_desc(slot, k, n, off), cond)

    def g_wait(slot, k, cond=None):
        b = plan[k][0]

        def act():
            for n, off in enumerate(plan[k][1]):
                q = flip(flip(elem, off), b)
                remote(hist.at[slot, q], hist.at[slot, q], g_s.at[slot, k, n], g_r.at[slot, k, n],
                       elem=flip(elem, b)).wait_recv()
        act() if cond is None else pl.when(cond)(act)

    last = len(bits) - 1

    def g_rest(slot, cond=None):
        for k in range(len(bits)):
            g_wait(slot, k, cond)
            if k < last:
                g_start(slot, k + 1, cond)

    def z_desc(j):
        slot = STEPS - 2 - j
        return remote(past_h.at[depth - 1 - j, :, pl.ds(pl.multiple_of(elem * cols, cols), cols)],
                      hist.at[slot, elem], z_s.at[j], z_r.at[j], lag=up)

    for j in range(STEPS - 1):
        go(z_desc(j), inner)

    def mm(slot, i):
        acc = None
        for q in range(n_elem):
            term = nt(hist[slot, q], kern[i, :, q * cols:(q + 1) * cols])
            acc = term if acc is None else acc + term
        return acc

    lane = lax.broadcasted_iota(jnp.int32, (scen, cols), 1) + elem * cols
    begin = patch[...]
    weakening = WEAKEN * flags[...].astype(jnp.float32)

    @pl.when(first)
    def _():
        slip[...] = initial[...]

    def v_desc(t, c):
        part = hist.at[NEW + t, elem, pl.ds(c * crow, crow), :]
        return remote(part, part, v_s.at[t, c], v_r.at[t, c], lag=up)

    def relay_rate(t):
        for c in range(CHUNKS):
            pl.when(later)(v_desc(t, c).wait_recv)
            go(v_desc(t, c), inner & later)
        g_start(NEW + t, 0, later)

    for t in range(STEPS):
        acc = None
        for i in range(t, depth):
            if t == 0:
                for c in pcopies[i]:
                    c.wait()
                kcopies[i].wait()
            term = mm(STEPS - 1 + i - t, i)
            acc = term if acc is None else acc + term
        for i in range(1, t):
            acc = acc + mm(jnp.where(first, NEW + t - 1 - i, STEPS - 1 + i - t), i)
        psum[t] = acc
        if t:
            slot = STEPS - 1 - t
            g_rest(slot, later)
            g_rest(NEW + t - 1, first)
            psum[t] += mm(jnp.where(first, NEW + t - 1, slot), 0)
        if t < STEPS - 1:
            pl.when(later)(z_desc(t).wait_recv)
            g_start(STEPS - 2 - t, 0, later)
        for c in range(CHUNKS):
            span = pl.ds(c * crow, crow)

            def chain(c=c, span=span, t=t):
                remote(psum.at[t, span, :], pin.at[t, span, :], p_s.at[t, c], p_r.at[t, c], lag=down).wait_recv()
                psum[t, span, :] += pin[t, span, :]
            pl.when(inner)(chain)
            go(remote(psum.at[t, span, :], pin.at[t, span, :], p_s.at[t, c], p_r.at[t, c], lag=down), later)

        @pl.when(first)
        def _(t=t):
            inside = jnp.where((lane >= begin) & (lane < begin + PATCH), 1.0, 0.0).astype(jnp.float32)
            traction = loading[...] + OVERSTRESS * inside + psum[t]
            now = slip[...]
            strength = peak[...] * (1.0 - weakening * now / (now + CRITICAL))
            rate = jnp.maximum(traction - strength, 0.0).astype(jnp.bfloat16)
            slip[...] = now + rate.astype(jnp.float32)
            hist[NEW + t, elem] = rate
            if t == STEPS - 1:
                for d in range(n_lag):
                    trs[d] = traction[d * rows:(d + 1) * rows]
        g_start(NEW + t, 0, first)
        for c in range(CHUNKS):
            go(v_desc(t, c), first & inner)

        if t == 0:
            for h in range(handlers):
                go(remote(rad_h.at[pl.ds(STEPS + h * depth, depth)], radin.at[lag],
                          rad_s.at[h], rad_r.at[lag], lag=h), lag != h)
                go(remote(bpad, bin_v.at[lag], bm_s.at[h], bm_r.at[lag], lag=h), lag != h)
        if t >= 2:
            relay_rate(t - 2)
    for t in range(2, STEPS):
        relay_rate(t)

    def t_desc(k):
        d = lax.rem(lag + k, n_lag)
        return remote(trs.at[d], trin, t_s.at[d], t_r, lag=d)

    @pl.when(first)
    def _():
        lax.fori_loop(1, n_lag, lambda k, c: (t_desc(k).start(), c)[1], 0)

    rcopy.wait()

    recv = motion_out.shape[0]
    width = kernel_h.shape[2] // SBLK
    per = cols // width

    def radiate(kernels, slots, blocks):
        masks = [[jnp.broadcast_to(blocks[0:1, k:k + 1], (recv, width)) == b for k in range(near)]
                 for b in range(SBLK)]
        acc = jnp.zeros((recv, scen), jnp.float32)
        for get, slot in zip(kernels, slots):
            value = get().astype(jnp.float32)
            for q in range(n_elem):
                spread = []
                for b in range(q * per, (q + 1) * per):
                    block = jnp.zeros((recv, width), jnp.float32)
                    for k in range(near):
                        block = jnp.where(masks[b][k], value[:, k * width:(k + 1) * width], block)
                    spread.append(block)
                acc = acc + nt(jnp.concatenate(spread, axis=1).astype(jnp.bfloat16), hist[slot, q])
        return acc

    @pl.when(lag < handlers)
    def _():
        def one(k, c):
            d = lax.rem(lag + k, n_lag)
            remote(rad_h.at[pl.ds(0, depth)], radin.at[d], rad_s.at[0], rad_r.at[d], lag=0).wait_recv()
            remote(bpad, bin_v.at[d], bm_s.at[0], bm_r.at[d], lag=0).wait_recv()
            mpart[d] = radiate([lambda j=j: radin[d, j] for j in range(depth)],
                               [STEPS - 1 + j for j in range(depth)], bin_v[d])
            remote(mpart.at[d], min_.at[lag], m_s.at[d], m_r.at[lag], lag=d).start()
            return c
        lax.fori_loop(1, n_lag, one, 0)
        min_[lag] = radiate([lambda j=j: rad[STEPS + lag * depth + j] for j in range(depth)],
                            [STEPS - 1 + j for j in range(depth)], bpad[...])

    for t in range(STEPS):
        cond = later if t < STEPS - 1 else None
        g_rest(NEW + t, cond)
    motion_out[...] = radiate([lambda m=m: rad[m] for m in range(STEPS)],
                              [NEW + STEPS - 1 - m for m in range(STEPS)], bpad[...])

    whole = initial[...]
    for t in range(STEPS):
        whole = whole + hist[NEW + t, elem].astype(jnp.float32)
    for d in range(n_lag):
        @pl.when(lag == d)
        def _(d=d):
            slip_out[...] = whole[d * rows:(d + 1) * rows]

    @pl.when(first)
    def _():
        trac_out[...] = trs[0]

    @pl.when(later)
    def _():
        remote(trs.at[0], trin, t_s.at[0], t_r, lag=0).wait_recv()
        trac_out[...] = trin[...]

    for h in range(handlers):
        @pl.when(lag != h)
        def _(h=h):
            remote(mpart.at[0], min_.at[h], m_s.at[0], m_r.at[h], lag=h).wait_recv()
        motion_out[...] += min_[h]

    for cond, desc in pending:
        if cond is None:
            desc.wait_send()
        else:
            pl.when(cond)(desc.wait_send)

    @pl.when(first)
    def _():
        lax.fori_loop(1, n_lag, lambda k, c: (t_desc(k).wait_send(), c)[1], 0)

    @pl.when(lag < handlers)
    def _():
        def one(k, c):
            d = lax.rem(lag + k, n_lag)
            remote(mpart.at[d], min_.at[lag], m_s.at[d], m_r.at[lag], lag=d).wait_send()
            return c
        lax.fori_loop(1, n_lag, one, 0)


def on_device(n_lag, n_elem, kernel, past_rate, loading, initial_slip, peak_strength, cohesive_flags, patch_start,
              rad_kernel, block_map):
    depth, cols, _ = kernel.shape
    scen = past_rate.shape[1]
    lags, recv, wide = rad_kernel.shape
    rows = scen // n_lag
    handlers = (lags - STEPS) // depth
    nbits = n_elem.bit_length() - 1
    bpad = jnp.zeros((8, 128), jnp.int32).at[:1, :block_map.shape[1]].set(block_map)
    f32, bf16 = jnp.float32, jnp.bfloat16
    dma = pltpu.SemaphoreType.DMA
    vmem = pl.BlockSpec(memory_space=pltpu.VMEM)
    hbm = pl.BlockSpec(memory_space=pl.ANY)
    slots = 2 * STEPS - 1 + depth
    slip, traction, motion = pl.pallas_call(
        functools.partial(body, n_lag, n_elem, block_map.shape[1]),
        out_shape=(
            jax.ShapeDtypeStruct((rows, cols), f32),
            jax.ShapeDtypeStruct((rows, cols), f32),
            jax.ShapeDtypeStruct((recv, scen), f32),
        ),
        in_specs=[hbm, hbm, vmem, vmem, vmem, vmem, vmem, hbm, vmem],
        out_specs=(vmem, vmem, vmem),
        scratch_shapes=[
            pltpu.VMEM((depth, cols, kernel.shape[2]), bf16),
            pltpu.VMEM((slots, n_elem, scen, cols), bf16),
            pltpu.VMEM((lags, recv, wide), bf16),
            pltpu.VMEM((n_lag, depth, recv, wide), bf16),
            pltpu.VMEM((n_lag, 8, 128), jnp.int32),
            pltpu.VMEM((STEPS, scen, cols), f32),
            pltpu.VMEM((STEPS, scen, cols), f32),
            pltpu.VMEM((scen, cols), f32),
            pltpu.VMEM((n_lag, rows, cols), f32),
            pltpu.VMEM((rows, cols), f32),
            pltpu.VMEM((n_lag, recv, scen), f32),
            pltpu.VMEM((max(handlers, 1), recv, scen), f32),
            dma((depth,)), dma((depth, n_elem)), dma,
            dma((STEPS,)), dma((STEPS,)),
            dma((slots, nbits, n_elem)), dma((slots, nbits, n_elem)),
            dma((STEPS, CHUNKS)), dma((STEPS, CHUNKS)),
            dma((STEPS, CHUNKS)), dma((STEPS, CHUNKS)),
            dma((handlers,)), dma((n_lag,)),
            dma((handlers,)), dma((n_lag,)),
            dma((n_lag,)), dma,
            dma((n_lag,)), dma((n_lag,)),
        ],
        compiler_params=pltpu.CompilerParams(
            collective_id=0, has_side_effects=True, vmem_limit_bytes=60 * 1024 * 1024),
    )(kernel, past_rate, loading, initial_slip, peak_strength[None], cohesive_flags[None], patch_start[:, None],
      rad_kernel, bpad)
    return slip, traction, motion.T


def solution(mesh):
    n_lag, n_elem = mesh.shape["lag"], mesh.shape["elem"]
    return jax.shard_map(
        functools.partial(on_device, n_lag, n_elem),
        mesh=mesh,
        in_specs=(
            P("lag", "elem", None),
            P("lag", "scen", None),
            P("scen", "elem"),
            P("scen", "elem"),
            P("elem"),
            P("elem"),
            P("scen"),
            P(None, ("lag", "elem"), None),
            P(("lag", "elem"), None),
        ),
        out_specs=(
            P(("scen", "lag"), "elem"),
            P(("scen", "lag"), "elem"),
            P("scen", ("lag", "elem")),
        ),
        check_vma=False,
    )
```

time: 448 us -> 113 us (0.25)
  waiting for transfers between devices: 243 us -> 0 us
  Pallas kernels: 0 us -> 105 us
  blocking collectives: 93.8 us -> 0 us
  matrix products: 31.5 us -> 0 us
  local copies, waits for them, and re-layouts: 37.4 us -> 6.96 us
  other arithmetic: 14.3 us -> 0 us
  between operations: 14.1 us -> 0.64 us
  starting transfers between devices: 9.53 us -> 0 us
    psum x1 -> x0, waiting for transfers between devices: 200 us -> none  [from_root(): return lax.psum(jnp.where(mine, value, jnp.zeros_like(value)), axis)]
    pallas_call x0 -> x1, Pallas kernels: none -> 105 us  [on_device(): pl.pallas_call(functools.partial(body, n_lag, n_elem, block_map.shape[1])...]
    all_gather x8 -> x0, blocking collectives: 93.8 us -> none  [the longest x4 61.8 us: on_device(): gathered = lax.all_gather(gathered, 'lag', axis=0, tiled=True)]
    reduce_scatter x4 -> x0, waiting for transfers between devices: 43.6 us -> none  [on_device(): lax.psum_scatter(partial_value, 'lag', scatter_dimension=0, tiled=True)]
    dot_general x8 -> x0, matrix products: 31.5 us -> none  [the longest x4 28.9 us: lag_terms(): lax.dot_general(history, kernel, (((0, 2), (0, 2)), ((), ())), preferred_...]
    reshape x3 -> x0, local copies, waits for them, and re-layouts: 10.7 us -> none  [select_blocks(): rate_block.reshape(rate_block.shape[0], rate_block.shape[1], SBLK, rate_b...]
    gather x4 -> x0, local copies, waits for them, and re-layouts: 10.4 us -> none  [select_blocks(): chosen = jnp.take(grouped, sources, axis=2)]
    ppermute x3 -> x0, starting transfers between devices: 9.15 us -> none  [shifted(): lax.ppermute(value, axis, [(source, source + steps) for source in range(f...]
  transfers between devices with their start and end apart: 8 -> 0, of which waited for: 5 -> 0; matrix products, arithmetic and copies ran while one was open for 7% -> 0% of each run, Pallas kernels for 0% -> 0%
where the time goes in v1:
time: 113 us; the launch traced here: 112 us
  Pallas kernels  105 us (93%)
  local copies, waits for them, and re-layouts  6.96 us (6%)
    pallas_call x1, Pallas kernels, on_device(): pl.pallas_call(functools.partial(body, n_lag, n_elem, block_map.shape[1])...  105 us
    unnamed x3, local copies, waits for them, and re-layouts  4.32 us

profile of v1, /device:TPU:19, one launch (start us, length us, event | category | flops | bytes accessed | tf_op | source)
XLA Modules:
  0.0 112.1 jit_solution(3599157155502436817)
XLA Ops:
  0.6 1.3 %scatter.4.bpad = s32[8,128]{1,0:T(8,128)} pad(s32[1,4]{1,0:T(1,128)} %param.19, s32[]{:T(128)} %constant.26.clone.1), padding=0_7x0_124 | pad | bytes 4116 | tf_op jit(solution)/shard_map/scatter | solution.py:323
  1.9 1.4 %copy.12.patch = s32[128,1]{1,0:T(8,128)} copy(s32[128,1]{0,1:T(1,128)} %bitcast.7) | data formatting | bytes 1024 | tf_op jit(solution)/shard_map/broadcast_in_dim | solution.py:363
  3.3 104.5 %shard_map.112 = (f32[32,512]{1,0:T(8,128)}, f32[32,512]{1,0:T(8,128)}, f32[64,128]{1,0:T(8,128)}) custom-call(bf16[4,512,2048]{2,1,0:T(8,128)(2,1)} %kernel_h.1, bf16[4,128,2048]{2,1,0:T(8,128)(2,1)} %past_h.1, f32[128,512]{1,0:T(8,128)} %loading.1, f32[128,512]{1,0:T(8,128)} %initial.1, f32[1,512]{1,0:T(1,128)} %bitcast.5, s32[1,512]{1,0:T(1,128)} %bitcast.6, ...), custom_call_target="tpu_custom_call" | custom-call | tf_op jit(solution)/shard_map/pallas_call | solution.py:329
  107.8 1.5 %copy.16 = f32[32,512]{1,0:T(8,128)} copy(f32[32,512]{1,0:T(8,128)} %get-tuple-element.24) | data formatting | bytes 131072
  109.3 1.5 %copy.17 = f32[32,512]{1,0:T(8,128)} copy(f32[32,512]{1,0:T(8,128)} %get-tuple-element.25) | data formatting | bytes 131072
  110.7 1.4 %copy.18 = f32[128,64]{0,1:T(8,128)} copy(f32[128,64]{0,1:T(8,128)} %bitcast.4) | data formatting | bytes 65536

commit v2 on v1

--- a/solution.py
+++ b/solution.py
@@ -14,7 +14,8 @@
 WEAKEN = 0.5
 CRITICAL = 0.5
 
-CHUNKS = 2
+CHUNKS = 4
+LEVELS = 32767.0
 
 
 def flip(e, bits):
@@ -34,9 +35,9 @@
     n_lag, n_elem, near,
     kernel_h, past_h, loading, initial, peak, flags, patch, rad_h, bpad,
     slip_out, trac_out, motion_out,
-    kern, hist, rad, radin, bin_v, psum, pin, slip, trs, trin, mpart, min_,
+    kern, hist, rad, radin, bin_v, psum, pout, pin, sout, sin, slip, trs, trin, mpart, min_,
     ksem, psem, rsem,
-    z_s, z_r, g_s, g_r, p_s, p_r, v_s, v_r, rad_s, rad_r, bm_s, bm_r, t_s, t_r, m_s, m_r,
+    z_s, z_r, g_s, g_r, p_s, p_r, q_s, q_r, v_s, v_r, rad_s, rad_r, bm_s, bm_r, t_s, t_r, m_s, m_r,
 ):
     depth, cols, _ = kern.shape
     scen = psum.shape[1]
@@ -188,11 +189,24 @@
         for c in range(CHUNKS):
             span = pl.ds(c * crow, crow)
 
-            def chain(c=c, span=span, t=t):
-                remote(psum.at[t, span, :], pin.at[t, span, :], p_s.at[t, c], p_r.at[t, c], lag=down).wait_recv()
-                psum[t, span, :] += pin[t, span, :]
-            pl.when(inner)(chain)
-            go(remote(psum.at[t, span, :], pin.at[t, span, :], p_s.at[t, c], p_r.at[t, c], lag=down), later)
+            def moves(c=c, span=span, t=t):
+                return (remote(pout.at[t, span, :], pin.at[t, span, :], p_s.at[t, c], p_r.at[t, c], lag=down),
+                        remote(sout.at[t, c], sin.at[t, c], q_s.at[t, c], q_r.at[t, c], lag=down))
+
+            @pl.when(inner)
+            def _(moves=moves, c=c, span=span, t=t):
+                for move in moves():
+                    move.wait_recv()
+                psum[t, span, :] += pin[t, span, :].astype(jnp.int32).astype(jnp.float32) * sin[t, c, 0:1, 0:1]
+
+            @pl.when(later)
+            def _(c=c, span=span, t=t):
+                value = psum[t, span, :]
+                top = jnp.maximum(jnp.max(jnp.abs(value), axis=(0, 1), keepdims=True), 1e-30)
+                pout[t, span, :] = jnp.floor(value * (LEVELS / top) + 0.5).astype(jnp.int32).astype(jnp.int16)
+                sout[t, c] = jnp.broadcast_to(top / LEVELS, sout.shape[2:])
+            for move in moves():
+                go(move, later)
 
         @pl.when(first)
         def _(t=t):
@@ -342,7 +356,10 @@
             pltpu.VMEM((n_lag, depth, recv, wide), bf16),
             pltpu.VMEM((n_lag, 8, 128), jnp.int32),
             pltpu.VMEM((STEPS, scen, cols), f32),
-            pltpu.VMEM((STEPS, scen, cols), f32),
+            pltpu.VMEM((STEPS, scen, cols), jnp.int16),
+            pltpu.VMEM((STEPS, scen, cols), jnp.int16),
+            pltpu.VMEM((STEPS, CHUNKS, 8, 128), f32),
+            pltpu.VMEM((STEPS, CHUNKS, 8, 128), f32),
             pltpu.VMEM((scen, cols), f32),
             pltpu.VMEM((n_lag, rows, cols), f32),
             pltpu.VMEM((rows, cols), f32),
@@ -351,6 +368,7 @@
             dma((depth,)), dma((depth, n_elem)), dma,
             dma((STEPS,)), dma((STEPS,)),
             dma((slots, nbits, n_elem)), dma((slots, nbits, n_elem)),
+            dma((STEPS, CHUNKS)), dma((STEPS, CHUNKS)),
             dma((STEPS, CHUNKS)), dma((STEPS, CHUNKS)),
             dma((STEPS, CHUNKS)), dma((STEPS, CHUNKS)),
             dma((handlers,)), dma((n_lag,)),

time: 113 us -> 101 us (0.89)
  Pallas kernels: 105 us -> 92.4 us
    pallas_call x1, Pallas kernels: 105 us -> 92.4 us  [on_device(): pl.pallas_call(functools.partial(body, n_lag, n_elem, block_map.shape[1])...]
where the time goes in v2:
time: 101 us; the launch traced here: 100 us
  Pallas kernels  92.4 us (91%)
  local copies, waits for them, and re-layouts  6.96 us (7%)
    pallas_call x1, Pallas kernels, on_device(): pl.pallas_call(functools.partial(body, n_lag, n_elem, block_map.shape[1])...  92.4 us
    unnamed x3, local copies, waits for them, and re-layouts  4.32 us

profile of v2, /device:TPU:19, one launch (start us, length us, event | category | flops | bytes accessed | tf_op | source)
XLA Modules:
  0.0 100.0 jit_solution(9029209655871010490)
XLA Ops:
  0.6 1.3 %scatter.4.bpad = s32[8,128]{1,0:T(8,128)} pad(s32[1,4]{1,0:T(1,128)} %param.19, s32[]{:T(128)} %constant.26.clone.1), padding=0_7x0_124 | pad | bytes 4116 | tf_op jit(solution)/shard_map/scatter | solution.py:337
  1.9 1.4 %copy.12.patch = s32[128,1]{1,0:T(8,128)} copy(s32[128,1]{0,1:T(1,128)} %bitcast.7) | data formatting | bytes 1024 | tf_op jit(solution)/shard_map/broadcast_in_dim | solution.py:381
  3.3 92.4 %shard_map.112 = (f32[32,512]{1,0:T(8,128)}, f32[32,512]{1,0:T(8,128)}, f32[64,128]{1,0:T(8,128)}) custom-call(bf16[4,512,2048]{2,1,0:T(8,128)(2,1)} %kernel_h.1, bf16[4,128,2048]{2,1,0:T(8,128)(2,1)} %past_h.1, f32[128,512]{1,0:T(8,128)} %loading.1, f32[128,512]{1,0:T(8,128)} %initial.1, f32[1,512]{1,0:T(1,128)} %bitcast.5, s32[1,512]{1,0:T(1,128)} %bitcast.6, ...), custom_call_target="tpu_custom_call" | custom-call | tf_op jit(solution)/shard_map/pallas_call | solution.py:343
  95.7 1.5 %copy.16 = f32[32,512]{1,0:T(8,128)} copy(f32[32,512]{1,0:T(8,128)} %get-tuple-element.24) | data formatting | bytes 131072
  97.2 1.5 %copy.17 = f32[32,512]{1,0:T(8,128)} copy(f32[32,512]{1,0:T(8,128)} %get-tuple-element.25) | data formatting | bytes 131072
  98.6 1.4 %copy.18 = f32[128,64]{0,1:T(8,128)} copy(f32[128,64]{0,1:T(8,128)} %bitcast.4) | data formatting | bytes 65536

commit v3 on v2

--- a/solution.py
+++ b/solution.py
@@ -32,12 +32,12 @@
 
 
 def body(
-    n_lag, n_elem, near,
+    n_lag, n_elem, n_scen, near,
     kernel_h, past_h, loading, initial, peak, flags, patch, rad_h, bpad,
     slip_out, trac_out, motion_out,
-    kern, hist, rad, radin, bin_v, psum, pout, pin, sout, sin, slip, trs, trin, mpart, min_,
+    kern, hist, rad, radin, bin_v, psum, pout, pin, sout, sin, slip, trs, trin, rrs, rrin, rz, mpart, min_,
     ksem, psem, rsem,
-    z_s, z_r, g_s, g_r, p_s, p_r, q_s, q_r, v_s, v_r, rad_s, rad_r, bm_s, bm_r, t_s, t_r, m_s, m_r,
+    z_s, z_r, g_s, g_r, p_s, p_r, q_s, q_r, v_s, v_r, rad_s, rad_r, bm_s, bm_r, t_s, t_r, m_s, m_r, r_s, r_r, rz_s, rz_r, y_s, y_r,
 ):
     depth, cols, _ = kern.shape
     scen = psum.shape[1]
@@ -47,6 +47,9 @@
     handlers = (rad_h.shape[0] - STEPS) // depth
     lag = lax.axis_index("lag")
     elem = lax.axis_index("elem")
+    scn = lax.axis_index("scen")
+    other = lax.rem(scn + 1, n_scen)
+    half = depth // n_scen
     first = lag == 0
     later = lag > 0
     inner = lag < n_lag - 1
@@ -93,7 +96,8 @@
     for b in bits:
         pl.semaphore_signal(barrier, inc=1, device_id={"elem": flip(elem, b)},
                             device_id_type=pl.DeviceIdType.MESH)
-    pl.semaphore_wait(barrier, n_lag - 1 + len(bits))
+    pl.semaphore_signal(barrier, inc=1, device_id={"scen": other}, device_id_type=pl.DeviceIdType.MESH)
+    pl.semaphore_wait(barrier, n_lag + len(bits))
 
     def stages():
         held = [0]
@@ -220,27 +224,42 @@
             if t == STEPS - 1:
                 for d in range(n_lag):
                     trs[d] = traction[d * rows:(d + 1) * rows]
+                    rrs[d] = rate[d * rows:(d + 1) * rows]
         g_start(NEW + t, 0, first)
-        for c in range(CHUNKS):
-            go(v_desc(t, c), first & inner)
-
-        if t == 0:
+        if t < STEPS - 1:
+            for c in range(CHUNKS):
+                go(v_desc(t, c), first & inner)
+
+        if t == 1:
+            go(remote(rad_h.at[0], rz.at[lag], rz_s, rz_r.at[lag], lag=0), later)
             for h in range(handlers):
-                go(remote(rad_h.at[pl.ds(STEPS + h * depth, depth)], radin.at[lag],
+                go(remote(bpad, bin_v.at[lag], bm_s.at[h], bm_r.at[lag], lag=h), lag != h)
+                go(remote(rad_h.at[pl.ds(STEPS + h * depth + scn * half, half)],
+                          radin.at[lag, pl.ds(scn * half, half)],
                           rad_s.at[h], rad_r.at[lag], lag=h), lag != h)
-                go(remote(bpad, bin_v.at[lag], bm_s.at[h], bm_r.at[lag], lag=h), lag != h)
         if t >= 2:
             relay_rate(t - 2)
-    for t in range(2, STEPS):
+    for t in range(2, STEPS - 1):
         relay_rate(t)
 
     def t_desc(k):
         d = lax.rem(lag + k, n_lag)
         return remote(trs.at[d], trin, t_s.at[d], t_r, lag=d)
 
-    @pl.when(first)
-    def _():
-        lax.fori_loop(1, n_lag, lambda k, c: (t_desc(k).start(), c)[1], 0)
+    def r_desc(k):
+        d = lax.rem(lag + k, n_lag)
+        return remote(rrs.at[d], rrin, r_s.at[d], r_r, lag=d)
+
+    def y_desc(d, side):
+        part = radin.at[d, pl.ds(side * half, half)]
+        return remote(part, part, y_s.at[d], y_r.at[d], scen=other)
+
+    def m_desc(d):
+        return remote(mpart.at[d], min_.at[lag], m_s.at[d], m_r.at[lag], lag=d)
+
+    @pl.when(first)
+    def _():
+        lax.fori_loop(1, n_lag, lambda k, c: (t_desc(k).start(), r_desc(k).start(), c)[2], 0)
 
     rcopy.wait()
 
@@ -266,31 +285,60 @@
 
     @pl.when(lag < handlers)
     def _():
+        def share(k, c):
+            d = lax.rem(lag + k, n_lag)
+            part = radin.at[d, pl.ds(scn * half, half)]
+            remote(part, part, rad_s.at[0], rad_r.at[d], lag=0).wait_recv()
+            y_desc(d, scn).start()
+            return c
+        lax.fori_loop(1, n_lag, share, 0)
+        min_[lag] = radiate([lambda j=j: rad[STEPS + lag * depth + j] for j in range(depth)],
+                            [STEPS - 1 + j for j in range(depth)], bpad[...])
+
         def one(k, c):
             d = lax.rem(lag + k, n_lag)
-            remote(rad_h.at[pl.ds(0, depth)], radin.at[d], rad_s.at[0], rad_r.at[d], lag=0).wait_recv()
+            y_desc(d, other).wait_recv()
             remote(bpad, bin_v.at[d], bm_s.at[0], bm_r.at[d], lag=0).wait_recv()
             mpart[d] = radiate([lambda j=j: radin[d, j] for j in range(depth)],
                                [STEPS - 1 + j for j in range(depth)], bin_v[d])
-            remote(mpart.at[d], min_.at[lag], m_s.at[d], m_r.at[lag], lag=d).start()
+            pl.when(later)(m_desc(d).start)
             return c
         lax.fori_loop(1, n_lag, one, 0)
-        min_[lag] = radiate([lambda j=j: rad[STEPS + lag * depth + j] for j in range(depth)],
-                            [STEPS - 1 + j for j in range(depth)], bpad[...])
-
-    for t in range(STEPS):
-        cond = later if t < STEPS - 1 else None
-        g_rest(NEW + t, cond)
-    motion_out[...] = radiate([lambda m=m: rad[m] for m in range(STEPS)],
-                              [NEW + STEPS - 1 - m for m in range(STEPS)], bpad[...])
-
-    whole = initial[...]
-    for t in range(STEPS):
-        whole = whole + hist[NEW + t, elem].astype(jnp.float32)
-    for d in range(n_lag):
-        @pl.when(lag == d)
-        def _(d=d):
-            slip_out[...] = whole[d * rows:(d + 1) * rows]
+
+    g_rest(NEW + STEPS - 1, first)
+
+    @pl.when(first)
+    def _():
+        def one(k, c):
+            d = lax.rem(lag + k, n_lag)
+            remote(rz.at[d], rz.at[d], rz_s, rz_r.at[d], lag=0).wait_recv()
+            mpart[d] += radiate([lambda: rz[d]], [NEW + STEPS - 1], bin_v[d])
+            m_desc(d).start()
+            return c
+        lax.fori_loop(1, n_lag, one, 0)
+    for t in range(STEPS - 1):
+        g_rest(NEW + t, later)
+    motion_out[...] = radiate([lambda m=m: rad[m] for m in range(1, STEPS)],
+                              [NEW + STEPS - 1 - m for m in range(1, STEPS)], bpad[...])
+
+    @pl.when(first)
+    def _():
+        motion_out[...] += radiate([lambda: rad[0]], [NEW + STEPS - 1], bpad[...])
+
+    @pl.when(first)
+    def _():
+        slip_out[...] = slip[0:rows]
+
+    @pl.when(later)
+    def _():
+        remote(rrs.at[0], rrin, r_s.at[0], r_r, lag=0).wait_recv()
+        whole = initial[...]
+        for t in range(STEPS - 1):
+            whole = whole + hist[NEW + t, elem].astype(jnp.float32)
+        for d in range(1, n_lag):
+            @pl.when(lag == d)
+            def _(d=d):
+                slip_out[...] = whole[d * rows:(d + 1) * rows] + rrin[...].astype(jnp.float32)
 
     @pl.when(first)
     def _():
@@ -315,18 +363,19 @@
 
     @pl.when(first)
     def _():
-        lax.fori_loop(1, n_lag, lambda k, c: (t_desc(k).wait_send(), c)[1], 0)
+        lax.fori_loop(1, n_lag, lambda k, c: (t_desc(k).wait_send(), r_desc(k).wait_send(), c)[2], 0)
 
     @pl.when(lag < handlers)
     def _():
         def one(k, c):
             d = lax.rem(lag + k, n_lag)
-            remote(mpart.at[d], min_.at[lag], m_s.at[d], m_r.at[lag], lag=d).wait_send()
+            y_desc(d, scn).wait_send()
+            m_desc(d).wait_send()
             return c
         lax.fori_loop(1, n_lag, one, 0)
 
 
-def on_device(n_lag, n_elem, kernel, past_rate, loading, initial_slip, peak_strength, cohesive_flags, patch_start,
+def on_device(n_lag, n_elem, n_scen, kernel, past_rate, loading, initial_slip, peak_strength, cohesive_flags, patch_start,
               rad_kernel, block_map):
     depth, cols, _ = kernel.shape
     scen = past_rate.shape[1]
@@ -341,7 +390,7 @@
     hbm = pl.BlockSpec(memory_space=pl.ANY)
     slots = 2 * STEPS - 1 + depth
     slip, traction, motion = pl.pallas_call(
-        functools.partial(body, n_lag, n_elem, block_map.shape[1]),
+        functools.partial(body, n_lag, n_elem, n_scen, block_map.shape[1]),
         out_shape=(
             jax.ShapeDtypeStruct((rows, cols), f32),
             jax.ShapeDtypeStruct((rows, cols), f32),
@@ -363,6 +412,9 @@
             pltpu.VMEM((scen, cols), f32),
             pltpu.VMEM((n_lag, rows, cols), f32),
             pltpu.VMEM((rows, cols), f32),
+            pltpu.VMEM((n_lag, rows, cols), bf16),
+            pltpu.VMEM((rows, cols), bf16),
+            pltpu.VMEM((n_lag, recv, wide), bf16),
             pltpu.VMEM((n_lag, recv, scen), f32),
             pltpu.VMEM((max(handlers, 1), recv, scen), f32),
             dma((depth,)), dma((depth, n_elem)), dma,
@@ -375,6 +427,8 @@
             dma((handlers,)), dma((n_lag,)),
             dma((n_lag,)), dma,
             dma((n_lag,)), dma((n_lag,)),
+            dma((n_lag,)), dma, dma, dma((n_lag,)),
+            dma((n_lag,)), dma((n_lag,)),
         ],
         compiler_params=pltpu.CompilerParams(
             collective_id=0, has_side_effects=True, vmem_limit_bytes=60 * 1024 * 1024),
@@ -386,7 +440,7 @@
 def solution(mesh):
     n_lag, n_elem = mesh.shape["lag"], mesh.shape["elem"]
     return jax.shard_map(
-        functools.partial(on_device, n_lag, n_elem),
+        functools.partial(on_device, n_lag, n_elem, mesh.shape["scen"]),
         mesh=mesh,
         in_specs=(
             P("lag", "elem", None),

time: 101 us -> 97.1 us (0.961)
  Pallas kernels: 92.4 us -> 89.2 us
    pallas_call x1, Pallas kernels: 92.4 us -> 89.2 us  [on_device(): pl.pallas_call(functools.partial(body, n_lag, n_elem, n_scen, block_map.s...]
where the time goes in v3:
time: 97.1 us; the launch traced here: 96.8 us
  Pallas kernels  89.2 us (92%)
  local copies, waits for them, and re-layouts  6.96 us (7%)
    pallas_call x1, Pallas kernels, on_device(): pl.pallas_call(functools.partial(body, n_lag, n_elem, n_scen, block_map.s...  89.2 us
    unnamed x3, local copies, waits for them, and re-layouts  4.32 us

profile of v3, /device:TPU:19, one launch (start us, length us, event | category | flops | bytes accessed | tf_op | source)
XLA Modules:
  0.0 96.8 jit_solution(17820994450636168265)
XLA Ops:
  0.6 1.3 %scatter.4.bpad = s32[8,128]{1,0:T(8,128)} pad(s32[1,4]{1,0:T(1,128)} %param.19, s32[]{:T(128)} %constant.26.clone.1), padding=0_7x0_124 | pad | bytes 4116 | tf_op jit(solution)/shard_map/scatter | solution.py:386
  1.9 1.4 %copy.12.patch = s32[128,1]{1,0:T(8,128)} copy(s32[128,1]{0,1:T(1,128)} %bitcast.7) | data formatting | bytes 1024 | tf_op jit(solution)/shard_map/broadcast_in_dim | solution.py:435
  3.3 89.2 %shard_map.112 = (f32[32,512]{1,0:T(8,128)}, f32[32,512]{1,0:T(8,128)}, f32[64,128]{1,0:T(8,128)}) custom-call(bf16[4,512,2048]{2,1,0:T(8,128)(2,1)} %kernel_h.1, bf16[4,128,2048]{2,1,0:T(8,128)(2,1)} %past_h.1, f32[128,512]{1,0:T(8,128)} %loading.1, f32[128,512]{1,0:T(8,128)} %initial.1, f32[1,512]{1,0:T(1,128)} %bitcast.5, s32[1,512]{1,0:T(1,128)} %bitcast.6, ...), custom_call_target="tpu_custom_call" | custom-call | tf_op jit(solution)/shard_map/pallas_call | solution.py:392
  92.5 1.5 %copy.16 = f32[32,512]{1,0:T(8,128)} copy(f32[32,512]{1,0:T(8,128)} %get-tuple-element.24) | data formatting | bytes 131072
  94.0 1.5 %copy.17 = f32[32,512]{1,0:T(8,128)} copy(f32[32,512]{1,0:T(8,128)} %get-tuple-element.25) | data formatting | bytes 131072
  95.4 1.4 %copy.18 = f32[128,64]{0,1:T(8,128)} copy(f32[128,64]{0,1:T(8,128)} %bitcast.4) | data formatting | bytes 65536

commit v4 on v3

--- a/solution.py
+++ b/solution.py
@@ -230,7 +230,7 @@
             for c in range(CHUNKS):
                 go(v_desc(t, c), first & inner)
 
-        if t == 1:
+        if t == STEPS - 1:
             go(remote(rad_h.at[0], rz.at[lag], rz_s, rz_r.at[lag], lag=0), later)
             for h in range(handlers):
                 go(remote(bpad, bin_v.at[lag], bm_s.at[h], bm_r.at[lag], lag=h), lag != h)
@@ -383,7 +383,7 @@
     rows = scen // n_lag
     handlers = (lags - STEPS) // depth
     nbits = n_elem.bit_length() - 1
-    bpad = jnp.zeros((8, 128), jnp.int32).at[:1, :block_map.shape[1]].set(block_map)
+    bpad = jnp.pad(block_map, ((0, 7), (0, 128 - block_map.shape[1])))
     f32, bf16 = jnp.float32, jnp.bfloat16
     dma = pltpu.SemaphoreType.DMA
     vmem = pl.BlockSpec(memory_space=pltpu.VMEM)

time: 97.1 us -> 96.1 us (0.990)
  Pallas kernels: 89.2 us -> 88 us
    pad x0 -> x1, local copies, waits for them, and re-layouts: none -> 1.25 us  [on_device(): bpad = jnp.pad(block_map, ((0, 7), (0, 128 - block_map.shape[1])))]
    scatter x1 -> x0, local copies, waits for them, and re-layouts: 1.25 us -> none  [on_device(): jnp.zeros((8, 128), jnp.int32).at[:1, :block_map.shape[1]].set(block_map)]
    pallas_call x1, Pallas kernels: 89.2 us -> 88 us  [on_device(): pl.pallas_call(functools.partial(body, n_lag, n_elem, n_scen, block_map.s...]
where the time goes in v4:
time: 96.1 us; the launch traced here: 95.6 us
  Pallas kernels  88 us (92%)
  local copies, waits for them, and re-layouts  6.96 us (7%)
    pallas_call x1, Pallas kernels, on_device(): pl.pallas_call(functools.partial(body, n_lag, n_elem, n_scen, block_map.s...  88 us
    unnamed x3, local copies, waits for them, and re-layouts  4.32 us

profile of v4, /device:TPU:19, one launch (start us, length us, event | category | flops | bytes accessed | tf_op | source)
XLA Modules:
  0.0 95.6 jit_solution(2334590995411090581)
XLA Ops:
  0.6 1.3 %pad.4.bpad = s32[8,128]{1,0:T(8,128)} pad(s32[1,4]{1,0:T(1,128)} %param.17, s32[]{:T(128)} %constant.0.clone.1), padding=0_7x0_124 | pad | bytes 4116 | tf_op jit(solution)/shard_map/jit(_pad)/pad | solution.py:386
  1.9 1.4 %copy.12.patch = s32[128,1]{1,0:T(8,128)} copy(s32[128,1]{0,1:T(1,128)} %bitcast.7) | data formatting | bytes 1024 | tf_op jit(solution)/shard_map/broadcast_in_dim | solution.py:435
  3.3 88.0 %shard_map.112 = (f32[32,512]{1,0:T(8,128)}, f32[32,512]{1,0:T(8,128)}, f32[64,128]{1,0:T(8,128)}) custom-call(bf16[4,512,2048]{2,1,0:T(8,128)(2,1)} %kernel_h.1, bf16[4,128,2048]{2,1,0:T(8,128)(2,1)} %past_h.1, f32[128,512]{1,0:T(8,128)} %loading.1, f32[128,512]{1,0:T(8,128)} %initial.1, f32[1,512]{1,0:T(1,128)} %bitcast.5, s32[1,512]{1,0:T(1,128)} %bitcast.6, ...), custom_call_target="tpu_custom_call" | custom-call | tf_op jit(solution)/shard_map/pallas_call | solution.py:392
  91.3 1.5 %copy.16 = f32[32,512]{1,0:T(8,128)} copy(f32[32,512]{1,0:T(8,128)} %get-tuple-element.12) | data formatting | bytes 131072
  92.7 1.5 %copy.17 = f32[32,512]{1,0:T(8,128)} copy(f32[32,512]{1,0:T(8,128)} %get-tuple-element.13) | data formatting | bytes 131072
  94.2 1.4 %copy.18 = f32[128,64]{0,1:T(8,128)} copy(f32[128,64]{0,1:T(8,128)} %bitcast.4) | data formatting | bytes 65536
